TPU v7x, 32 devices: a whole 2x2x4 slice. The times are simulated.
32 devices in a mesh: grp: 2 (over y), seq: 4 (over x, core), lab: 4 (over z).
Axes of the slice: x: 2, y: 2, z: 4, core: 2. Of those that a mesh axis runs over, the one named last changes fastest.
Arguments:
- hidden: bfloat16 [6144, 4096], P(('grp', 'seq'), 'lab'), parts along dimension 0, may hold values from -6 to 6
- proj_weight: bfloat16 [4096, 256], P('lab'), may hold values from -0.09375 to 0.09375
- queries: bfloat16 [9216, 256], P('lab'), may hold values from -0.25 to 0.25
- code_weight: bfloat16 [9216, 256], P('lab'), may hold values from -4 to 4
- code_bias: float32 [9216], P('lab'), may hold values from -0.5 to 0.5
- labels: int32 [4, 9216], P('grp', 'lab'), parts along dimension 0, may hold values 0 or 1
- code_counts: int32 [8, 9216], P(('grp', 'seq'), 'lab'), parts along dimension 0, may hold values from 0 to 119, as said below
Outputs:
- note_loss: float32 [4], P('grp'), parts along dimension 0
- grad_hidden: bfloat16 [6144, 4096], P(('grp', 'seq'), 'lab'), parts along dimension 0
- grad_proj: bfloat16 [8192, 256], P(('grp', 'lab', 'seq')), parts along dimension 0
- grad_queries: bfloat16 [18432, 256], P(('grp', 'lab', 'seq')), parts along dimension 0
- grad_code_weight: bfloat16 [18432, 256], P(('grp', 'lab', 'seq')), parts along dimension 0
- grad_bias: float32 [18432], P(('grp', 'lab')), parts along dimension 0
There are 2 independent parts, one for each index of `grp`. A program takes and returns all parts, laid end to end along the dimension named above; an argument that names none is the same for every part. Nothing has to cross between parts.
Inputs may be any that keep to these rules, and one draw needn't show every extreme that they name: `code_counts`: entry (i, c) counts the occurrences of code c in the part of the training corpus read by loader i.
All inputs are finite; a program needn't handle non-finite values. No bound on the sum of `labels` on one device may be relied on, other than what follows from the above.
Results may differ from a plain program's by a relative error of at most 0.025.
Values may be sent and summed in bfloat16 or wider, within the bound.
A program may use at most 64 MiB of HBM per device.

v0:
```python
import math
import jax
import jax.numpy as jnp
from jax import lax
from jax.sharding import PartitionSpec as P

balance_beta = 0.9999


def focal_loss(logit, target):
    prob = jax.nn.sigmoid(logit)
    return -(
        target * (1.0 - prob) * (1.0 - prob) * jax.nn.log_sigmoid(logit)
        + (1.0 - target) * prob * prob * jax.nn.log_sigmoid(-logit)
    )


def rounded(value):
    return lax.optimization_barrier(value.astype(jnp.bfloat16)).astype(jnp.float32)


def per_device(hidden, proj_weight, queries, code_weight, code_bias, labels, code_counts):
    lab_count = lax.axis_size("lab")
    seq_count = lax.axis_size("seq")
    note_count = labels.shape[0]
    all_codes = queries.shape[0] * lab_count
    pre_part = lax.psum_scatter(
        jnp.dot(hidden, proj_weight, preferred_element_type=jnp.float32).astype(jnp.bfloat16),
        "lab",
        scatter_dimension=0,
        tiled=True,
    ).astype(jnp.float32)
    latent_share = jnp.tanh(pre_part).astype(jnp.bfloat16)
    latent = lax.all_gather(latent_share, "lab", axis=0, tiled=True)
    scores = jnp.einsum("te,ce->tc", latent, queries, preferred_element_type=jnp.float32)
    values = jnp.einsum("te,ce->tc", latent, code_weight, preferred_element_type=jnp.float32)
    weights = jnp.exp(scores)
    note_here = lax.axis_index("seq") * note_count // seq_count
    note_pick = (jnp.arange(note_count, dtype=jnp.int32) == note_here).astype(jnp.float32)[:, None]
    den_local = jnp.sum(weights, 0)[None, :]
    num_local = jnp.sum(weights * values, 0)[None, :]
    counts_local = jnp.sum(code_counts.astype(jnp.float32), 0)
    denominator, numerator, counted = (
        lax.psum((note_pick * den_local).astype(jnp.bfloat16), "seq").astype(jnp.float32),
        lax.psum((note_pick * num_local).astype(jnp.bfloat16), "seq").astype(jnp.float32),
        lax.psum(counts_local.astype(jnp.bfloat16), "seq").astype(jnp.float32),
    )
    mean_value = numerator / denominator
    logits = mean_value + code_bias[None, :]
    occurrences = 1.0 + counted
    class_weight = (1.0 - balance_beta) / -jnp.expm1(occurrences * math.log(balance_beta))
    targets = labels.astype(jnp.float32)
    focal_value, pullback = jax.vjp(lambda point: focal_loss(point, targets), logits)
    focal_grad = pullback(jnp.ones_like(logits))[0]
    weight_total, weighted_loss = lax.psum(
        (jnp.sum(class_weight), jnp.sum(focal_value * class_weight[None, :], 1)), "lab"
    )
    factor = all_codes / weight_total
    note_loss = factor * weighted_loss
    logit_grad = factor * class_weight[None, :] * focal_grad
    grad_bias = jnp.sum(logit_grad, 0)
    grad_here = jnp.sum(note_pick * logit_grad, 0)[None, :]
    den_here = jnp.sum(note_pick * denominator, 0)[None, :]
    mean_here = jnp.sum(note_pick * mean_value, 0)[None, :]
    value_part = weights / den_here * grad_here
    score_part = value_part * (values - mean_here)
    value_grad = value_part.astype(jnp.bfloat16)
    score_grad = score_part.astype(jnp.bfloat16)
    first = jnp.dot(score_grad, queries, preferred_element_type=jnp.float32)
    grad_share = lax.psum_scatter(
        (first + jnp.dot(value_grad, code_weight, preferred_element_type=jnp.float32)).astype(
            jnp.bfloat16
        ),
        "lab",
        scatter_dimension=0,
        tiled=True,
    ).astype(jnp.float32)
    share_wide = latent_share.astype(jnp.float32)
    pre_share_grad = (grad_share * (1.0 - share_wide * share_wide)).astype(jnp.bfloat16)
    pre_grad = lax.all_gather(pre_share_grad, "lab", axis=0, tiled=True)
    grad_hidden = jnp.einsum(
        "te,de->td", pre_grad, proj_weight, preferred_element_type=jnp.float32
    ).astype(jnp.bfloat16)
    proj_part = jnp.einsum("td,te->de", hidden, pre_grad, preferred_element_type=jnp.float32)
    query_part = jnp.einsum("tc,te->ce", score_grad, latent, preferred_element_type=jnp.float32)
    weight_part = jnp.einsum("tc,te->ce", value_grad, latent, preferred_element_type=jnp.float32)
    query_sum, weight_sum, proj_sum = (
        lax.psum_scatter(
            rounded(query_part).astype(jnp.bfloat16), "seq", scatter_dimension=0, tiled=True
        ).astype(jnp.float32),
        lax.psum_scatter(
            rounded(weight_part).astype(jnp.bfloat16), "seq", scatter_dimension=0, tiled=True
        ).astype(jnp.float32),
        lax.psum_scatter(
            rounded(proj_part).astype(jnp.bfloat16), "seq", scatter_dimension=0, tiled=True
        ).astype(jnp.float32),
    )
    return (
        note_loss,
        grad_hidden,
        proj_sum.astype(jnp.bfloat16),
        query_sum.astype(jnp.bfloat16),
        weight_sum.astype(jnp.bfloat16),
        grad_bias,
    )


def solution(mesh):
    placed = (
        P(("grp", "seq"), "lab"),
        P("lab", None),
        P("lab", None),
        P("lab", None),
        P("lab"),
        P("grp", "lab"),
        P(("grp", "seq"), "lab"),
    )
    return jax.shard_map(
        per_device,
        mesh=mesh,
        in_specs=placed,
        out_specs=(
            P("grp"),
            P(("grp", "seq"), "lab"),
            P(("grp", "lab", "seq"), None),
            P(("grp", "lab", "seq"), None),
            P(("grp", "lab", "seq"), None),
            P(("grp", "lab")),
        ),
        check_vma=False,
    )
```

profile of v0, /device:TPU:0, one launch (start us, length us, event | category | flops | bytes accessed | tf_op | source)
XLA Modules:
  0.0 211.3 jit_solution(14797629354521924660)
XLA Ops:
  7.2 1.4 copy-done
  8.6 2.4 %convolution_convert_fusion.4 = bf16[768,256]{1,0:T(8,128)(2,1)} fusion(bf16[768,1024]{1,0:T(8,128)(2,1)S(1)} %copy-done, bf16[1024,256]{1,0:T(8,128)(2,1)} %param.9), kind=kOutput, calls=%fused_computation.11 | convolution fusion | flops 402849792 | bytes 2490368 | tf_op jit(solution)/shard_map/dot_general | solution.py:28
  11.0 0.7 convert_reduce_fusion
  11.8 22.6 %reduce-scatter.6.cloned.1.call-done = bf16[192,256]{1,0:T(8,128)(2,1)} async-done(((bf16[768,256]{1,0:T(8,128)(2,1)}), bf16[192,256]{1,0:T(8,128)(2,1)}) %reduce-scatter.6.cloned.1.call-update) | async-done | bytes 98320 | tf_op jit(solution)/shard_map/reduce_scatter | solution.py:27
  34.4 0.9 tanh_convert_fusion
  35.3 14.8 %all_gather.6 = bf16[768,256]{1,0:T(8,128)(2,1)S(1)} all-gather(bf16[192,256]{1,0:T(8,128)(2,1)S(1)} %tanh_convert_fusion), channel_id=1, replica_groups=mesh['grp'=2,'seq'=4,'lab'=4] {'lab'}, dimensions={0}, use_global_device_ids=true | all-gather | bytes 491520 | tf_op jit(solution)/shard_map/all_gather | solution.py:34
  50.2 2.5 %fusion.17 = f32[768,2304]{1,0:T(8,128)S(1)} fusion(bf16[768,256]{1,0:T(8,128)(2,1)S(1)} %all_gather.6, bf16[2304,256]{1,0:T(8,128)(2,1)} %param.10), kind=kOutput, calls=%fused_computation.52 | convolution fusion | flops 905969664 | bytes 8650752 | tf_op jit(solution)/shard_map/te,ce->tc/dot_general | solution.py:35
  52.7 4.8 %multiply_reduce_fusion = (f32[2304]{0:T(1024)S(1)}, f32[2304]{0:T(1024)S(1)}, f32[768,2304]{1,0:T(8,128)}) fusion(f32[768,2304]{1,0:T(8,128)S(1)} %fusion.17, bf16[768,256]{1,0:T(8,128)(2,1)S(1)} %all_gather.6, bf16[2304,256]{1,0:T(8,128)(2,1)S(1)} %copy-done.4), kind=kOutput, calls=%fused_computation.2 | convolution fusion | flops 911273472 | bytes 15747072 | tf_op jit(solution)/shard_map/te,ce->tc/dot_general | solution.py:36
  57.5 0.2 copy-done.1
  57.6 0.1 multiply_convert_fusion.3
  57.7 10.3 %all-reduce = (bf16[2304]{0:T(1024)(128)(2,1)S(1)}, bf16[2,2304]{1,0:T(2,128)(2,1)S(1)}, bf16[2,2304]{1,0:T(2,128)(2,1)S(1)}) all-reduce(bf16[2304]{0:T(1024)(128)(2,1)S(1)} %convert_reduce_fusion, bf16[2,2304]{1,0:T(2,128)(2,1)S(1)} %get-tuple-element.39, ...), channel_id=1, replica_groups=mesh['grp'=2,'seq'=4,'lab'=4] {'seq'}, use_global_device_ids=true, to_apply=%region_0.0 | all-reduce | flops 11520 | bytes 46080 | tf_op jit(solution)/shard_map/psum | solution.py:46
  68.0 0.6 negate_divide_fusion
  68.6 9.0 %psum.36 = f32[]{:T(128)} all-reduce(f32[]{:T(128)} %get-tuple-element.37), channel_id=1, replica_groups=mesh['grp'=2,'seq'=4,'lab'=4] {'lab'}, use_global_device_ids=true, to_apply=%region_2.3 | all-reduce | flops 1 | bytes 8 | tf_op jit(solution)/shard_map/psum | solution.py:55
  78.3 0.2 fusion.14
  78.5 0.8 fusion.16
  79.4 6.0 %fusion = (bf16[768,2304]{1,0:T(8,128)(2,1)S(1)}, bf16[768,2304]{1,0:T(8,128)(2,1)S(1)}) fusion(f32[2304]{0:T(1024)S(1)} %get-tuple-element.23, f32[2304]{0:T(1024)S(1)} %get-tuple-element.26, f32[768,2304]{1,0:T(8,128)} %copy-done.1, f32[768,2304]{1,0:T(8,128)} %get-tuple-element.40, f32[2304]{0:T(1024)S(1)} %get-tuple-element.28), kind=kLoop, calls=%fused_computation.6 | loop fusion | flops 10616832 | bytes 21261312 | tf_op jit(solution)/shard_map/convert_element_type | solution.py:67
  85.4 1.8 copy-done.3
  87.2 1.1 fusion.18
  88.3 1.8 fusion.1
  90.2 20.2 %reduce-scatter.8.cloned.1.call-done = bf16[192,256]{1,0:T(8,128)(2,1)} async-done(((bf16[768,256]{1,0:T(8,128)(2,1)}), bf16[192,256]{1,0:T(8,128)(2,1)}) %reduce-scatter.8.cloned.1.call-update) | async-done | bytes 98320 | tf_op jit(solution)/shard_map/reduce_scatter | solution.py:70
  110.4 0.9 multiply_convert_fusion.1
  111.3 14.8 %all_gather.7 = bf16[768,256]{1,0:T(8,128)(2,1)S(1)} all-gather(bf16[192,256]{1,0:T(8,128)(2,1)S(1)} %multiply_convert_fusion.1), channel_id=1, replica_groups=mesh['grp'=2,'seq'=4,'lab'=4] {'lab'}, dimensions={0}, use_global_device_ids=true | all-gather | bytes 491520 | tf_op jit(solution)/shard_map/all_gather | solution.py:80
  126.1 1.4 fusion.2
  127.6 4.2 %convolution_convert_fusion.1 = bf16[2304,256]{1,0:T(8,128)(2,1)} fusion(bf16[768,2304]{1,0:T(8,128)(2,1)} %copy-done.3, bf16[768,256]{1,0:T(8,128)(2,1)S(1)} %all_gather.6), kind=kOutput, calls=%fused_computation.5 | convolution fusion | flops 906559488 | bytes 5111808 | tf_op jit(solution)/shard_map/tc,te->ce/dot_general | solution.py:85
  131.9 4.3 %convolution_convert_fusion = bf16[2304,256]{1,0:T(8,128)(2,1)} fusion(bf16[768,2304]{1,0:T(8,128)(2,1)} %copy-done.2, bf16[768,256]{1,0:T(8,128)(2,1)S(1)} %all_gather.6), kind=kOutput, calls=%fused_computation.4 | convolution fusion | flops 906559488 | bytes 5111808 | tf_op jit(solution)/shard_map/tc,te->ce/dot_general | solution.py:86
  136.2 8.4 %psum.39 = f32[2]{0:T(128)S(1)} all-reduce(f32[2]{0:T(128)S(1)} %get-tuple-element.27), channel_id=1, replica_groups=mesh['grp'=2,'seq'=4,'lab'=4] {'lab'}, use_global_device_ids=true, to_apply=%region_9.11 | all-reduce | flops 2 | bytes 16 | tf_op jit(solution)/shard_map/psum | solution.py:55
  144.6 0.5 broadcast_multiply_fusion.1
  145.1 1.7 convolution_convert_fusion.2
  146.8 0.3 reduce-scatter.10.cloned.1.call-done
  147.1 1.7 copy.13
  148.8 27.2 %reduce-scatter.12.cloned.1.call-done = bf16[576,256]{1,0:T(8,128)(2,1)} async-done(((bf16[2304,256]{1,0:T(8,128)(2,1)}), bf16[576,256]{1,0:T(8,128)(2,1)}) %reduce-scatter.12.cloned.1.call-update) | async-done | bytes 294928 | tf_op jit(solution)/shard_map/reduce_scatter | solution.py:88
  176.0 28.7 %reduce-scatter.14.cloned.1.call-done = bf16[576,256]{1,0:T(8,128)(2,1)} async-done(((bf16[2304,256]{1,0:T(8,128)(2,1)}), bf16[576,256]{1,0:T(8,128)(2,1)}) %reduce-scatter.14.cloned.1.call-update) | async-done | bytes 294928 | tf_op jit(solution)/shard_map/reduce_scatter | solution.py:91
  (29 shorter events, 0.4 us)
Async XLA Ops:
  7.2 1.4 copy-start
  7.2 27.2 %reduce-scatter.6.cloned.1.call-start = ((), (), s32[]{:S(2)}) async-start(), calls=%async_computation.5 | async-start | bytes 491520 | tf_op jit(solution)/shard_map/reduce_scatter | solution.py:27
  11.0 99.4 %reduce-scatter.8.cloned.1.call-start = ((), (), s32[]{:S(2)}) async-start(), calls=%async_computation.6 | async-start | bytes 491520 | tf_op jit(solution)/shard_map/reduce_scatter | solution.py:70
  50.1 2.5 %copy-start.4 = (bf16[2304,256]{1,0:T(8,128)(2,1)S(1)}, bf16[2304,256]{1,0:T(8,128)(2,1)}, u32[]{:S(2)}) copy-start(bf16[2304,256]{1,0:T(8,128)(2,1)} %param.11) | copy-start | bytes 3538948
  52.6 5.0 %copy-start.1 = (f32[768,2304]{1,0:T(8,128)}, f32[768,2304]{1,0:T(8,128)S(1)}, u32[]{:S(2)}) copy-start(f32[768,2304]{1,0:T(8,128)S(1)} %fusion.17) | copy-start | bytes 21233668
  52.7 25.6 %copy-start.8 = (s32[2,2304]{1,0:T(2,128)S(1)}, s32[2,2304]{1,0:T(2,128)}, u32[]{:S(2)}) copy-start(s32[2,2304]{1,0:T(2,128)} %param.13) | copy-start | bytes 55300
  52.7 25.6 %copy-start.9 = (f32[2304]{0:T(1024)S(1)}, f32[2304]{0:T(1024)}, u32[]{:S(2)}) copy-start(f32[2304]{0:T(1024)} %param.12) | copy-start | bytes 27652
  79.4 7.9 %copy-start.5 = (bf16[2304,256]{1,0:T(8,128)(2,1)S(1)}, bf16[2304,256]{1,0:T(8,128)(2,1)}, u32[]{:S(2)}) copy-start(bf16[2304,256]{1,0:T(8,128)(2,1)} %param.10) | copy-start | bytes 3538948
  85.4 1.8 copy-start.3
  85.4 2.9 %copy-start.2 = (bf16[768,2304]{1,0:T(8,128)(2,1)}, bf16[768,2304]{1,0:T(8,128)(2,1)S(1)}, u32[]{:S(2)}) copy-start(bf16[768,2304]{1,0:T(8,128)(2,1)S(1)} %get-tuple-element.34) | copy-start | bytes 10616836
  88.3 22.1 %copy-start.7 = (bf16[192,256]{1,0:T(8,128)(2,1)S(1)}, bf16[192,256]{1,0:T(8,128)(2,1)}, u32[]{:S(2)}) copy-start(bf16[192,256]{1,0:T(8,128)(2,1)} %reduce-scatter.6.cloned.1.call-done) | copy-start | bytes 294916
  90.2 56.9 %reduce-scatter.10.cloned.1.call-start = ((), (), s32[]{:S(2)}) async-start(), calls=%async_computation.7 | async-start | bytes 655360 | tf_op jit(solution)/shard_map/reduce_scatter | solution.py:94
  127.6 48.4 %reduce-scatter.12.cloned.1.call-start = ((), (), s32[]{:S(2)}) async-start(), calls=%async_computation.8 | async-start | bytes 1474560 | tf_op jit(solution)/shard_map/reduce_scatter | solution.py:88
  131.8 13.3 %copy-start.6 = (bf16[1024,256]{1,0:T(8,128)(2,1)S(1)}, bf16[1024,256]{1,0:T(8,128)(2,1)}, u32[]{:S(2)}) copy-start(bf16[1024,256]{1,0:T(8,128)(2,1)} %param.9) | copy-start | bytes 1572868
  131.8 72.9 %reduce-scatter.14.cloned.1.call-start = ((), (), s32[]{:S(2)}) async-start(), calls=%async_computation.9 | async-start | bytes 1474560 | tf_op jit(solution)/shard_map/reduce_scatter | solution.py:91
Sparse Core Ops, SparseCore 0:
  11.1 23.2 reduce-scatter.5
  90.3 20.0 reduce-scatter.7
  127.7 19.3 reduce-scatter.9
  150.3 25.6 reduce-scatter.11
  179.0 25.7 reduce-scatter.13
where the time goes:
time: 212 us; the launch traced here: 211 us
  waiting for transfers between devices  99.1 us (47%)
  blocking collectives  57.2 us (27%)
  matrix products  24.2 us (11%)
  between operations  14.6 us (7%)
  other arithmetic  10.9 us (5%)
  local copies, waits for them, and re-layouts  5.01 us (2%)
    reduce_scatter x1, waiting for transfers between devices, per_device(): lax.psum_scatter(rounded(weight_part).astype(jnp.bfloat16), 'seq', scatte...  28.7 us
    reduce_scatter x1, waiting for transfers between devices, per_device(): lax.psum_scatter(rounded(query_part).astype(jnp.bfloat16), 'seq', scatter...  27.2 us
    reduce_scatter x1, waiting for transfers between devices, per_device(): lax.psum_scatter(jnp.dot(hidden, proj_weight, preferred_element_type=jnp....  22.6 us
    reduce_scatter x1, waiting for transfers between devices, per_device(): lax.psum_scatter((first + jnp.dot(value_grad, code_weight, preferred_elem...  20.2 us
    psum x2, blocking collectives, per_device(): lax.psum((jnp.sum(class_weight), jnp.sum(focal_value * class_weight[None,...  17.3 us
    all_gather x1, blocking collectives, per_device(): latent = lax.all_gather(latent_share, 'lab', axis=0, tiled=True)  14.8 us
    all_gather x1, blocking collectives, per_device(): pre_grad = lax.all_gather(pre_share_grad, 'lab', axis=0, tiled=True)  14.8 us
    psum x1, blocking collectives, per_device(): lax.psum(counts_local.astype(jnp.bfloat16), 'seq').astype(jnp.float32)  10.3 us
  transfers between devices with their start and end apart: 5, of which 5 were waited for; matrix products, arithmetic and copies ran while one was open for 6% of the time, Pallas kernels for 0%

commit v1 on v0

--- a/solution.py
+++ b/solution.py
@@ -5,6 +5,10 @@
 from jax.sharding import PartitionSpec as P
 
 balance_beta = 0.9999
+
+
+def spread_panels(x0):
+    return jnp.sum(lax.all_gather(x0, "seq"), 0)
 
 
 def focal_loss(logit, target):
@@ -43,7 +47,7 @@
     denominator, numerator, counted = (
         lax.psum((note_pick * den_local).astype(jnp.bfloat16), "seq").astype(jnp.float32),
         lax.psum((note_pick * num_local).astype(jnp.bfloat16), "seq").astype(jnp.float32),
-        lax.psum(counts_local.astype(jnp.bfloat16), "seq").astype(jnp.float32),
+        spread_panels(counts_local.astype(jnp.bfloat16)).astype(jnp.float32),
     )
     mean_value = numerator / denominator
     logits = mean_value + code_bias[None, :]

time: 212 us -> 201 us (0.948)
  waiting for transfers between devices: 99.1 us -> 78 us
  blocking collectives: 57.2 us -> 67.3 us
    reduce_scatter x1, waiting for transfers between devices: 22.6 us -> 2.18 us  [per_device(): lax.psum_scatter(jnp.dot(hidden, proj_weight, preferred_element_type=jnp....]
    all_gather x0 -> x1, blocking collectives: none -> 6.16 us  [spread_panels(): return jnp.sum(lax.all_gather(x0, 'seq'), 0)]
    psum x2, blocking collectives: 17.3 us -> 21.6 us  [per_device(): lax.psum((jnp.sum(class_weight), jnp.sum(focal_value * class_weight[None,...]
  transfers between devices with their start and end apart: 5 -> 5, of which waited for: 5 -> 5; matrix products, arithmetic and copies ran while one was open for 6% -> 7% of each run, Pallas kernels for 0% -> 0%
where the time goes in v1:
time: 201 us; the launch traced here: 200 us
  waiting for transfers between devices  78 us (39%)
  blocking collectives  67.3 us (33%)
  matrix products  24.2 us (12%)
  between operations  14.6 us (7%)
  other arithmetic  11 us (5%)
  local copies, waits for them, and re-layouts  5.01 us (2%)
    reduce_scatter x1, waiting for transfers between devices, per_device(): lax.psum_scatter(rounded(weight_part).astype(jnp.bfloat16), 'seq', scatte...  28.7 us
    reduce_scatter x1, waiting for transfers between devices, per_device(): lax.psum_scatter(rounded(query_part).astype(jnp.bfloat16), 'seq', scatter...  27.2 us
    psum x2, blocking collectives, per_device(): lax.psum((jnp.sum(class_weight), jnp.sum(focal_value * class_weight[None,...  21.6 us
    reduce_scatter x1, waiting for transfers between devices, per_device(): lax.psum_scatter((first + jnp.dot(value_grad, code_weight, preferred_elem...  19.1 us
    all_gather x1, blocking collectives, per_device(): pre_grad = lax.all_gather(pre_share_grad, 'lab', axis=0, tiled=True)  14.7 us
    all_gather x1, blocking collectives, per_device(): latent = lax.all_gather(latent_share, 'lab', axis=0, tiled=True)  14.6 us
    psum x1, blocking collectives, per_device(): lax.psum((note_pick * den_local).astype(jnp.bfloat16), 'seq')  10.3 us
    all_gather x1, blocking collectives, spread_panels(): return jnp.sum(lax.all_gather(x0, 'seq'), 0)  6.16 us
  transfers between devices with their start and end apart: 5, of which 5 were waited for; matrix products, arithmetic and copies ran while one was open for 7% of the time, Pallas kernels for 0%

profile of v1, /device:TPU:0, one launch (start us, length us, event | category | flops | bytes accessed | tf_op | source)
XLA Modules:
  0.0 200.3 jit_solution(7117929174515972611)
XLA Ops:
  7.2 1.4 copy-done
  8.6 2.4 %convolution_convert_fusion.4 = bf16[768,256]{1,0:T(8,128)(2,1)} fusion(bf16[768,1024]{1,0:T(8,128)(2,1)S(1)} %copy-done, bf16[1024,256]{1,0:T(8,128)(2,1)} %param.9), kind=kOutput, calls=%fused_computation.11 | convolution fusion | flops 402849792 | bytes 2490368 | tf_op jit(solution)/shard_map/dot_general | solution.py:32
  11.0 0.7 convert_bitcast_fusion
  11.7 6.2 %all-gather = bf16[4,1,2304]{2,1,0:T(2,128)(2,1)S(1)} all-gather(bf16[1,1,2304]{2,1,0:T(2,128)(2,1)S(1)} %convert_bitcast_fusion), channel_id=1, replica_groups=mesh['grp'=2,'seq'=4,'lab'=4] {'seq'}, dimensions={0}, use_global_device_ids=true | all-gather | bytes 23040 | tf_op jit(solution)/shard_map/all_gather | solution.py:11
  18.0 0.6 negate_divide_fusion
  18.6 13.0 %psum.28 = f32[]{:T(128)} all-reduce(f32[]{:T(128)} %get-tuple-element.42), channel_id=1, replica_groups=mesh['grp'=2,'seq'=4,'lab'=4] {'lab'}, use_global_device_ids=true, to_apply=%region_2.3 | all-reduce | flops 1 | bytes 8 | tf_op jit(solution)/shard_map/psum | solution.py:59
  32.4 2.2 %reduce-scatter.6.cloned.1.call-done = bf16[192,256]{1,0:T(8,128)(2,1)} async-done(((bf16[768,256]{1,0:T(8,128)(2,1)}), bf16[192,256]{1,0:T(8,128)(2,1)}) %reduce-scatter.6.cloned.1.call-update) | async-done | bytes 98320 | tf_op jit(solution)/shard_map/reduce_scatter | solution.py:31
  34.5 0.9 tanh_convert_fusion
  35.5 14.6 %all_gather.11 = bf16[768,256]{1,0:T(8,128)(2,1)S(1)} all-gather(bf16[192,256]{1,0:T(8,128)(2,1)S(1)} %tanh_convert_fusion), channel_id=1, replica_groups=mesh['grp'=2,'seq'=4,'lab'=4] {'lab'}, dimensions={0}, use_global_device_ids=true | all-gather | bytes 491520 | tf_op jit(solution)/shard_map/all_gather | solution.py:38
  50.1 2.5 %fusion.17 = f32[768,2304]{1,0:T(8,128)S(1)} fusion(bf16[768,256]{1,0:T(8,128)(2,1)S(1)} %all_gather.11, bf16[2304,256]{1,0:T(8,128)(2,1)} %param.10), kind=kOutput, calls=%fused_computation.52 | convolution fusion | flops 905969664 | bytes 8650752 | tf_op jit(solution)/shard_map/te,ce->tc/dot_general | solution.py:39
  52.6 4.8 %multiply_reduce_fusion = (f32[2304]{0:T(1024)S(1)}, f32[2304]{0:T(1024)S(1)}, f32[768,2304]{1,0:T(8,128)}) fusion(f32[768,2304]{1,0:T(8,128)S(1)} %fusion.17, bf16[768,256]{1,0:T(8,128)(2,1)S(1)} %all_gather.11, bf16[2304,256]{1,0:T(8,128)(2,1)S(1)} %copy-done.4), kind=kOutput, calls=%fused_computation.2 | convolution fusion | flops 911273472 | bytes 15747072 | tf_op jit(solution)/shard_map/te,ce->tc/dot_general | solution.py:40
  57.4 0.2 copy-done.1
  57.6 10.3 %all-reduce = (bf16[2,2304]{1,0:T(2,128)(2,1)S(1)}, bf16[2,2304]{1,0:T(2,128)(2,1)S(1)}) all-reduce(bf16[2,2304]{1,0:T(2,128)(2,1)S(1)} %get-tuple-element.44, bf16[2,2304]{1,0:T(2,128)(2,1)S(1)} %get-tuple-element.43), channel_id=1, replica_groups=mesh['grp'=2,'seq'=4,'lab'=4] {'seq'}, use_global_device_ids=true, to_apply=%region_7.8 | all-reduce | flops 9216 | bytes 36864 | tf_op jit(solution)/shard_map/psum | solution.py:48
  67.9 0.2 fusion.14
  68.1 0.8 fusion.16
  68.9 6.0 %fusion = (bf16[768,2304]{1,0:T(8,128)(2,1)S(1)}, bf16[768,2304]{1,0:T(8,128)(2,1)S(1)}) fusion(f32[2304]{0:T(1024)S(1)} %get-tuple-element.29, f32[2304]{0:T(1024)S(1)} %get-tuple-element.32, f32[768,2304]{1,0:T(8,128)} %copy-done.1, f32[768,2304]{1,0:T(8,128)} %get-tuple-element.45, f32[2304]{0:T(1024)S(1)} %get-tuple-element.34), kind=kLoop, calls=%fused_computation.6 | loop fusion | flops 10616832 | bytes 21261312 | tf_op jit(solution)/shard_map/convert_element_type | solution.py:71
  75.0 1.8 copy-done.3
  76.8 1.1 fusion.18
  77.9 1.8 fusion.1
  79.8 19.1 %reduce-scatter.8.cloned.1.call-done = bf16[192,256]{1,0:T(8,128)(2,1)} async-done(((bf16[768,256]{1,0:T(8,128)(2,1)}), bf16[192,256]{1,0:T(8,128)(2,1)}) %reduce-scatter.8.cloned.1.call-update) | async-done | bytes 98320 | tf_op jit(solution)/shard_map/reduce_scatter | solution.py:74
  99.0 0.9 multiply_convert_fusion.1
  99.9 14.7 %all_gather.12 = bf16[768,256]{1,0:T(8,128)(2,1)S(1)} all-gather(bf16[192,256]{1,0:T(8,128)(2,1)S(1)} %multiply_convert_fusion.1), channel_id=1, replica_groups=mesh['grp'=2,'seq'=4,'lab'=4] {'lab'}, dimensions={0}, use_global_device_ids=true | all-gather | bytes 491520 | tf_op jit(solution)/shard_map/all_gather | solution.py:84
  114.6 1.4 fusion.2
  116.2 4.2 %convolution_convert_fusion.1 = bf16[2304,256]{1,0:T(8,128)(2,1)} fusion(bf16[768,2304]{1,0:T(8,128)(2,1)} %copy-done.3, bf16[768,256]{1,0:T(8,128)(2,1)S(1)} %all_gather.11), kind=kOutput, calls=%fused_computation.5 | convolution fusion | flops 906559488 | bytes 5111808 | tf_op jit(solution)/shard_map/tc,te->ce/dot_general | solution.py:89
  120.4 4.3 %convolution_convert_fusion = bf16[2304,256]{1,0:T(8,128)(2,1)} fusion(bf16[768,2304]{1,0:T(8,128)(2,1)} %copy-done.2, bf16[768,256]{1,0:T(8,128)(2,1)S(1)} %all_gather.11), kind=kOutput, calls=%fused_computation.4 | convolution fusion | flops 906559488 | bytes 5111808 | tf_op jit(solution)/shard_map/tc,te->ce/dot_general | solution.py:90
  124.7 8.5 %psum.31 = f32[2]{0:T(128)S(1)} all-reduce(f32[2]{0:T(128)S(1)} %get-tuple-element.33), channel_id=1, replica_groups=mesh['grp'=2,'seq'=4,'lab'=4] {'lab'}, use_global_device_ids=true, to_apply=%region_9.11 | all-reduce | flops 2 | bytes 16 | tf_op jit(solution)/shard_map/psum | solution.py:59
  133.3 0.5 broadcast_multiply_fusion.1
  133.8 1.8 convolution_convert_fusion.2
  135.5 0.6 reduce-scatter.10.cloned.1.call-done
  136.1 1.7 copy.14
  137.8 27.2 %reduce-scatter.12.cloned.1.call-done = bf16[576,256]{1,0:T(8,128)(2,1)} async-done(((bf16[2304,256]{1,0:T(8,128)(2,1)}), bf16[576,256]{1,0:T(8,128)(2,1)}) %reduce-scatter.12.cloned.1.call-update) | async-done | bytes 294928 | tf_op jit(solution)/shard_map/reduce_scatter | solution.py:92
  165.0 28.7 %reduce-scatter.14.cloned.1.call-done = bf16[576,256]{1,0:T(8,128)(2,1)} async-done(((bf16[2304,256]{1,0:T(8,128)(2,1)}), bf16[576,256]{1,0:T(8,128)(2,1)}) %reduce-scatter.14.cloned.1.call-update) | async-done | bytes 294928 | tf_op jit(solution)/shard_map/reduce_scatter | solution.py:95
  (31 shorter events, 0.5 us)
Async XLA Ops:
  7.2 1.4 copy-start
  7.2 27.4 %reduce-scatter.6.cloned.1.call-start = ((), (), s32[]{:S(2)}) async-start(), calls=%async_computation.5 | async-start | bytes 491520 | tf_op jit(solution)/shard_map/reduce_scatter | solution.py:31
  11.0 88.0 %reduce-scatter.8.cloned.1.call-start = ((), (), s32[]{:S(2)}) async-start(), calls=%async_computation.6 | async-start | bytes 491520 | tf_op jit(solution)/shard_map/reduce_scatter | solution.py:74
  50.1 2.5 %copy-start.4 = (bf16[2304,256]{1,0:T(8,128)(2,1)S(1)}, bf16[2304,256]{1,0:T(8,128)(2,1)}, u32[]{:S(2)}) copy-start(bf16[2304,256]{1,0:T(8,128)(2,1)} %param.11) | copy-start | bytes 3538948
  52.5 5.0 %copy-start.1 = (f32[768,2304]{1,0:T(8,128)}, f32[768,2304]{1,0:T(8,128)S(1)}, u32[]{:S(2)}) copy-start(f32[768,2304]{1,0:T(8,128)S(1)} %fusion.17) | copy-start | bytes 21233668
  52.6 15.3 %copy-start.8 = (s32[2,2304]{1,0:T(2,128)S(1)}, s32[2,2304]{1,0:T(2,128)}, u32[]{:S(2)}) copy-start(s32[2,2304]{1,0:T(2,128)} %param.13) | copy-start | bytes 55300
  52.6 15.3 %copy-start.9 = (f32[2304]{0:T(1024)S(1)}, f32[2304]{0:T(1024)}, u32[]{:S(2)}) copy-start(f32[2304]{0:T(1024)} %param.12) | copy-start | bytes 27652
  68.9 7.9 %copy-start.5 = (bf16[2304,256]{1,0:T(8,128)(2,1)S(1)}, bf16[2304,256]{1,0:T(8,128)(2,1)}, u32[]{:S(2)}) copy-start(bf16[2304,256]{1,0:T(8,128)(2,1)} %param.10) | copy-start | bytes 3538948
  75.0 1.8 copy-start.3
  75.0 2.9 %copy-start.2 = (bf16[768,2304]{1,0:T(8,128)(2,1)}, bf16[768,2304]{1,0:T(8,128)(2,1)S(1)}, u32[]{:S(2)}) copy-start(bf16[768,2304]{1,0:T(8,128)(2,1)S(1)} %get-tuple-element.39) | copy-start | bytes 10616836
  77.9 21.1 %copy-start.7 = (bf16[192,256]{1,0:T(8,128)(2,1)S(1)}, bf16[192,256]{1,0:T(8,128)(2,1)}, u32[]{:S(2)}) copy-start(bf16[192,256]{1,0:T(8,128)(2,1)} %reduce-scatter.6.cloned.1.call-done) | copy-start | bytes 294916
  79.8 56.3 %reduce-scatter.10.cloned.1.call-start = ((), (), s32[]{:S(2)}) async-start(), calls=%async_computation.7 | async-start | bytes 655360 | tf_op jit(solution)/shard_map/reduce_scatter | solution.py:98
  116.1 48.9 %reduce-scatter.12.cloned.1.call-start = ((), (), s32[]{:S(2)}) async-start(), calls=%async_computation.8 | async-start | bytes 1474560 | tf_op jit(solution)/shard_map/reduce_scatter | solution.py:92
  120.3 13.4 %copy-start.6 = (bf16[1024,256]{1,0:T(8,128)(2,1)S(1)}, bf16[1024,256]{1,0:T(8,128)(2,1)}, u32[]{:S(2)}) copy-start(bf16[1024,256]{1,0:T(8,128)(2,1)} %param.9) | copy-start | bytes 1572868
  120.3 73.4 %reduce-scatter.14.cloned.1.call-start = ((), (), s32[]{:S(2)}) async-start(), calls=%async_computation.9 | async-start | bytes 1474560 | tf_op jit(solution)/shard_map/reduce_scatter | solution.py:95
Sparse Core Ops, SparseCore 0:
  11.1 23.4 reduce-scatter.5
  79.9 19.0 reduce-scatter.7
  116.2 19.8 reduce-scatter.9
  139.3 25.6 reduce-scatter.11
  168.0 25.7 reduce-scatter.13
